TPU v7x, 128 devices: a whole 4x4x4 slice. The times are simulated.
128 devices in a mesh: row: 4 (over y_lo, core), col: 32 (over y_hi, x, z).
Axes of the slice: x: 4, y: 4 (y_hi: 2, y_lo: 2; y = y_hi * 2 + y_lo), z: 4, core: 2. Of those that a mesh axis runs over, the one named last changes fastest.
Arguments:
- row_coords: bfloat16 [3, 4096, 512], P(None, ('row', 'col')), may hold values from -10 to 10, as said below
- col_coords: bfloat16 [3, 32768, 512], P(None, 'col'), may hold values from -10 to 10, as said below
- start_block: float32 [32768, 64], P('col'), may hold values from -0.03125 to 0.03125
Outputs:
- basis: float32 [4096, 64], P('row')
- image: float32 [32768, 64], P('col')
Inputs may be any that keep to these rules, and one draw needn't show every extreme that they name: `row_coords`: coordinates of frames of one molecule in varying conformations. `col_coords`: coordinates of frames of the same molecule in varying conformations.
All inputs are finite; a program needn't handle non-finite values.
Results may differ from a plain program's by a relative error of at most 0.0073.
Values may be sent and summed in bfloat16 or wider, within the bound.
No kernel may reach another device: no remote copies, remote signals or barrier semaphores. Data moves between devices by JAX's collectives and lax.ppermute only.
A program may use at most 128 MiB of HBM per device.

v0:
```python
import math
import jax
import jax.numpy as jnp
from jax import lax
from jax.sharding import PartitionSpec as P

ATOMS = 512
NEWTON = 8


def from_everyone(shard, axis):
    copies = jnp.broadcast_to(shard, (lax.axis_size(axis), *shard.shape))
    return lax.all_to_all(copies, axis, split_axis=0, concat_axis=0, tiled=True)


def over_copies(shard, axis):
    everything = from_everyone(shard, axis)
    return jnp.sum(everything, axis=0)


def filled_up(lines, devices):
    spare = -len(lines) % devices
    return jnp.pad(lines, [(0, spare)] + [(0, 0)] * (lines.ndim - 1))


def joined_along(pieces, dim):
    dims = list(pieces.shape[1:])
    dims[dim] *= pieces.shape[0]
    return jnp.moveaxis(pieces, 0, dim).reshape(dims)


def collect(shard, axis, dim):
    return joined_along(from_everyone(shard, axis), dim)


def cut_along(shard, dim, devices):
    dims = shard.shape
    pieces = shard.reshape(*dims[:dim], devices, dims[dim] // devices, *dims[dim + 1 :])
    return jnp.moveaxis(pieces, dim, 0)


def sum_at_owner(shard, axis, dim):
    pieces = cut_along(shard, dim, lax.axis_size(axis))
    arrived = lax.all_to_all(pieces, axis, split_axis=0, concat_axis=0, tiled=True)
    return arrived.sum(axis=0)


def total_of(shard, axes):
    padded = filled_up(shard, lax.axis_size(axes))
    whole = collect(sum_at_owner(padded, axes, 0), axes, 0)
    return lax.slice_in_dim(whole, 0, len(shard)).reshape(shard.shape)


def in_one(arrays, axis):
    ends = [0]
    for a in arrays:
        ends.append(ends[-1] + a.size)
    subtotal = total_of(jnp.concatenate([a.ravel() for a in arrays]), axis)
    return tuple((subtotal[b:e].reshape(a.shape) for a, b, e in zip(arrays, ends, ends[1:])))


def packed_total(arrays, axis):
    ends = [0]
    for a in arrays:
        ends.append(ends[-1] + a.size)
    subtotal = over_copies(jnp.concatenate([a.ravel() for a in arrays]), axis)
    return tuple((subtotal[b:e].reshape(a.shape) for a, b, e in zip(arrays, ends, ends[1:])))


def centre_frames(coords):
    shifted = coords.astype(jnp.float32)
    shifted = shifted - jnp.mean(shifted, axis=2, keepdims=True)
    rounded = shifted.astype(jnp.bfloat16)
    widened = lax.optimization_barrier(rounded).astype(jnp.float32)
    return (rounded, jnp.sum(widened * widened, axis=(0, 2)) / ATOMS)


def two_minor(matrix, upper, lower, left, right):
    return matrix[upper][left] * matrix[lower][right] - matrix[lower][left] * matrix[upper][right]


def squared_rmsd(cross, row_norm, col_norm):
    part = [[cross[first, second] for second in range(3)] for first in range(3)]
    trace = part[0][0] + part[1][1] + part[2][2]
    matrix = [[None] * 4 for index in range(4)]
    matrix[0][0] = trace
    matrix[1][1] = 2.0 * part[0][0] - trace
    matrix[2][2] = 2.0 * part[1][1] - trace
    matrix[3][3] = 2.0 * part[2][2] - trace
    matrix[0][1] = part[1][2] - part[2][1]
    matrix[0][2] = part[2][0] - part[0][2]
    matrix[0][3] = part[0][1] - part[1][0]
    matrix[1][2] = part[0][1] + part[1][0]
    matrix[1][3] = part[2][0] + part[0][2]
    matrix[2][3] = part[1][2] + part[2][1]
    for first in range(4):
        for second in range(first):
            matrix[first][second] = matrix[second][first]
    key_determinant = (
        two_minor(matrix, 0, 1, 0, 1) * two_minor(matrix, 2, 3, 2, 3)
        - two_minor(matrix, 0, 1, 0, 2) * two_minor(matrix, 2, 3, 1, 3)
        + two_minor(matrix, 0, 1, 0, 3) * two_minor(matrix, 2, 3, 1, 2)
        + two_minor(matrix, 0, 1, 1, 2) * two_minor(matrix, 2, 3, 0, 3)
        - two_minor(matrix, 0, 1, 1, 3) * two_minor(matrix, 2, 3, 0, 2)
        + two_minor(matrix, 0, 1, 2, 3) * two_minor(matrix, 2, 3, 0, 1)
    )
    cross_determinant = (
        part[0][0] * (part[1][1] * part[2][2] - part[1][2] * part[2][1])
        - part[0][1] * (part[1][0] * part[2][2] - part[1][2] * part[2][0])
        + part[0][2] * (part[1][0] * part[2][1] - part[1][1] * part[2][0])
    )
    squares = sum(
        (part[first][second] * part[first][second] for first in range(3) for second in range(3))
    )
    coeff_two = -2.0 * squares
    coeff_one = -8.0 * cross_determinant
    root_guess = 0.5 * (row_norm + col_norm)
    for sweep in range(NEWTON):
        poly_value = (
            (root_guess * root_guess + coeff_two) * root_guess + coeff_one
        ) * root_guess + key_determinant
        poly_slope = (4.0 * root_guess * root_guess + 2.0 * coeff_two) * root_guess + coeff_one
        root_guess = root_guess - poly_value / poly_slope
    return row_norm + col_norm - 2.0 * root_guess


def body(row_coords, col_coords, start_block):
    highest = lax.Precision.HIGHEST
    cols, col_norm = centre_frames(col_coords)
    rows, row_norm = centre_frames(lax.all_gather(row_coords, "col", axis=1, tiled=True))
    cross = jnp.einsum("ark,bck->abrc", rows, cols, preferred_element_type=jnp.float32) / ATOMS
    dist = squared_rmsd(cross, row_norm[:, None], col_norm[None, :])
    row_count, col_count = dist.shape
    total_rows = row_count * lax.axis_size("row")
    total_cols = col_count * lax.axis_size("col")
    block_mean = over_copies(jnp.sum(start_block, axis=0), "col") / total_cols
    panel_terms = (
        jnp.dot(dist, start_block - block_mean[None, :], precision=highest),
        jnp.sum(dist, axis=1),
    )
    summed = in_one((panel_terms[0], panel_terms[1]), "col")
    product = summed[0]
    stats = jax.tree.map(
        lambda part: over_copies(part, "row"),
        (jnp.dot(product.T, product, precision=highest), jnp.sum(product, axis=0)),
    )
    mean_row = stats[1] / total_rows
    panel = -0.5 * (summed[0] - mean_row[None, :])
    gram = 0.25 * (stats[0] / total_rows - jnp.outer(mean_row, mean_row))
    lower = jnp.linalg.cholesky(gram)
    basis = lax.linalg.triangular_solve(lower, panel, left_side=False, lower=True, transpose_a=True)
    row_totals = summed[1]
    column_terms = (
        jnp.dot(dist.T, basis, precision=highest),
        jnp.dot(row_totals, basis, precision=highest),
    )
    reduced = packed_total((column_terms[0], column_terms[1]), "row")
    image = -0.5 * (reduced[0] - reduced[1][None, :] / total_cols) / math.sqrt(total_rows)
    return (basis, image)


def solution(mesh):
    in_specs = (P(None, ("row", "col"), None), P(None, "col", None), P("col", None))
    out_specs = (P("row", None), P("col", None))
    return jax.shard_map(body, mesh=mesh, in_specs=in_specs, out_specs=out_specs, check_vma=False)
```

profile of v0, /device:TPU:1, one launch (start us, length us, event | category | flops | bytes accessed | tf_op | source)
XLA Modules:
  0.0 247.1 jit_solution(10567978950915025042)
XLA Ops:
  7.2 0.0 copy-start.1
  7.2 0.0 all-gather.2.cloned.1.call-start
  7.2 0.7 all-gather.2.cloned.1.call-update
  7.9 1.3 reduce_sum.112
  9.2 0.6 broadcast_in_dim.11
  9.8 11.3 %all-to-all-start = ((f32[32,1,64]{2,1,0:T(1,128)}), f32[32,1,64]{2,1,0:T(1,128)S(1)}, u32[]{:S(2)}, u32[]{:S(2)}) async-start(f32[32,1,64]{2,1,0:T(1,128)} %broadcast_in_dim.11), calls=%async_computation | async-start | bytes 32768 | tf_op jit(solution)/shard_map/all_to_all | solution.py:13
  21.1 2.4 convert_reduce_fusion
  23.5 0.0 copy-done.1
  23.6 0.8 fusion.7
  24.4 0.0 copy-start.3
  24.4 1.7 copy-done.3
  26.1 0.7 multiply_reduce_fusion
  26.8 3.0 %all-to-all-done = f32[32,1,64]{2,1,0:T(1,128)S(1)} async-done(((f32[32,1,64]{2,1,0:T(1,128)}), f32[32,1,64]{2,1,0:T(1,128)S(1)}, u32[]{:S(2)}, u32[]{:S(2)}) %all-to-all-start) | async-done | bytes 8224 | tf_op jit(solution)/shard_map/all_to_all | solution.py:13
  29.8 57.4 %all-gather.2.cloned.1.call-done = bf16[3,1024,512]{2,1,0:T(8,128)(2,1)} async-done(((bf16[3,32,512]{2,1,0:T(8,128)(2,1)}), bf16[3,1024,512]{2,1,0:T(8,128)(2,1)}) %all-gather.2.cloned.1.call-update) | async-done | bytes 3145744 | tf_op jit(solution)/shard_map/all_gather | solution.py:130
  87.2 0.0 copy-start.2
  87.2 2.5 %convert_reduce_fusion.1 = f32[3,1024]{1,0:T(4,128)S(1)} fusion(bf16[3,1024,512]{2,1,0:T(8,128)(2,1)} %all-gather.2.cloned.1.call-done), kind=kLoop, calls=%fused_computation.13 | loop fusion | flops 3142656 | bytes 3158016 | tf_op jit(solution)/shard_map/reduce_sum | solution.py:72
  89.7 0.3 copy-done.2
  90.0 0.8 fusion.6
  90.8 0.2 copy-done.4
  91.0 16.0 %multiply_bitcast_fusion = f32[3,3,1024,1024]{2,3,0,1:T(8,128)} fusion(bf16[3,1024,512]{2,1,0:T(8,128)(2,1)S(1)} %copy-done.4, bf16[3,1024,512]{2,1,0:T(8,128)(2,1)S(1)} %fusion.6), kind=kOutput, calls=%fused_computation | convolution fusion | flops 9673113600 | bytes 44040192 | tf_op jit(solution)/shard_map/ark,bck->abrc/dot_general | solution.py:131
  107.0 0.7 multiply_reduce_fusion.1
  107.7 0.0 copy-start.6
  107.7 35.8 %fusion.69 = (f32[1024]{0:T(1024)S(1)}, f32[1024,1024]{0,1:T(8,128)S(1)}) fusion(f32[3,3,1024,1024]{2,3,0,1:T(8,128)} %multiply_bitcast_fusion, f32[1024]{0:T(1024)S(1)} %broadcast_multiply_fusion.2, f32[1024]{0:T(1024)S(1)} %broadcast_multiply_fusion.3), kind=kLoop, calls=%fused_computation.119 | loop fusion | flops 210762752 | bytes 41955328 | tf_op jit(solution)/shard_map/reduce_sum | solution.py:139
  143.5 0.0 copy-start
  143.5 1.9 copy-done
  145.4 0.0 copy-done.6
  145.4 6.8 %fusion.61 = f32[1024,64]{1,0:T(8,128)S(1)} fusion(f32[1024,1024]{0,1:T(8,128)S(1)} %get-tuple-element.11, f32[1024,64]{0,1:T(8,128)S(1)} %copy-done.6, f32[64]{0:T(128)S(1)} %broadcast_multiply_fusion.5), kind=kOutput, calls=%fused_computation.96 | convolution fusion | flops 805371904 | bytes 4718848 | tf_op jit(solution)/shard_map/dot_general | solution.py:138
  152.2 0.1 reshape.82
  152.4 0.4 all_to_all.26
  152.7 14.3 %all_to_all.38 = f32[32,1,2080]{2,1,0:T(1,128)S(1)} all-to-all(f32[32,1,2080]{2,1,0:T(1,128)S(1)} %all_to_all.26), channel_id=1, replica_groups=mesh['row'=4,'col'=32] {'col'}, dimensions={0} | all-to-all | bytes 532480 | tf_op jit(solution)/shard_map/all_to_all | solution.py:44
  167.1 0.2 reduce_sum.115
  167.2 0.1 broadcast_in_dim.12
  167.4 12.9 %all_to_all.39 = f32[32,1,2080]{2,1,0:T(1,128)S(1)} all-to-all(f32[32,1,2080]{2,1,0:T(1,128)S(1)} %broadcast_in_dim.12), channel_id=1, replica_groups=mesh['row'=4,'col'=32] {'col'}, dimensions={0} | all-to-all | bytes 532480 | tf_op jit(solution)/shard_map/all_to_all | solution.py:13
  180.3 0.7 reduce.10
  181.0 0.2 slice.69
  181.2 0.2 slice_reduce_fusion
  181.4 0.6 broadcast_in_dim.14
  182.0 7.8 %all-to-all-start.3 = ((f32[4,1,64]{2,1,0:T(1,128)}), f32[4,1,64]{2,1,0:T(1,128)S(1)}, u32[]{:S(2)}, u32[]{:S(2)}) async-start(f32[4,1,64]{2,1,0:T(1,128)} %broadcast_in_dim.14), calls=%async_computation.3 | async-start | bytes 4096 | tf_op jit(solution)/shard_map/all_to_all | solution.py:13
  189.7 1.0 fusion.56
  190.8 0.2 reshape.84
  191.0 0.8 reshape.92
  191.8 1.0 all-to-all-done.3
  192.8 3.9 %all-to-all-start.4 = ((f32[4,1,4096]{2,1,0:T(1,128)}), f32[4,1,4096]{2,1,0:T(1,128)S(1)}, u32[]{:S(2)}, u32[]{:S(2)}) async-start(f32[4,1,4096]{2,1,0:T(1,128)} %reshape.92), calls=%async_computation.4 | async-start | bytes 131072 | tf_op jit(solution)/shard_map/all_to_all | solution.py:13
  196.7 3.2 %all-to-all-done.4 = f32[4,1,4096]{2,1,0:T(1,128)S(1)} async-done(((f32[4,1,4096]{2,1,0:T(1,128)}), f32[4,1,4096]{2,1,0:T(1,128)S(1)}, u32[]{:S(2)}, u32[]{:S(2)}) %all-to-all-start.4) | async-done | bytes 65568 | tf_op jit(solution)/shard_map/all_to_all | solution.py:13
  200.0 0.5 broadcast.147
  200.5 0.8 reduce.12
  201.3 0.1 reshape.93
  201.5 0.1 copy.62
  201.5 0.1 fusion.66
  201.6 5.8 %cholesky.16 = f32[64,64]{1,0:T(8,128)S(1)} custom-call(f32[64,64]{1,0:T(8,128)S(1)} %fusion.66), custom_call_target="Cholesky" | custom-call | tf_op jit(solution)/shard_map/jit(cholesky)/cholesky | solution.py:150
  207.5 0.6 compare_reduce_fusion
  208.1 0.7 fusion.64
  208.8 4.9 %custom-call.6 = f32[1,64,64]{1,2,0:T(8,128)S(1)} custom-call(f32[1,64,64]{2,1,0:T(8,128)S(1)} %fusion.64), custom_call_target="InvertDiagBlocksLowerTriangular" | custom-call | tf_op jit(solution)/shard_map/triangular_solve | solution.py:151
  213.7 0.8 fusion.53
  214.5 5.3 %fusion.70 = f32[1024,64]{1,0:T(8,128)S(1)} fusion(f32[1024,1024]{0,1:T(8,128)} %copy-done, f32[1024,64]{0,1:T(8,128)S(1)} %fusion.53), kind=kOutput, calls=%fused_computation.120 | convolution fusion | flops 805306368 | bytes 4718592 | tf_op jit(solution)/shard_map/dot_general | solution.py:154
  219.8 0.1 reshape.83
  219.9 0.3 convolution_bitcast_fusion
  220.2 0.1 pad_maximum_fusion.1
  220.3 0.5 broadcast_in_dim.30
  220.8 17.3 %all_to_all.40 = f32[4,1,65600]{2,1,0:T(1,128)S(1)} all-to-all(f32[4,1,65600]{2,1,0:T(1,128)S(1)} %broadcast_in_dim.30), channel_id=1, replica_groups=mesh['row'=4,'col'=32] {'row'}, dimensions={0} | all-to-all | bytes 2099200 | tf_op jit(solution)/shard_map/all_to_all | solution.py:13
  238.1 0.0 copy-done.5
  238.1 1.0 reduce_sum.119
  239.2 0.1 reshape.85
  239.4 0.9 copy.65
  (19 shorter events, 0.2 us)
Async XLA Ops:
  7.2 16.4 %copy-start.1 = (bf16[3,1024,512]{2,1,0:T(8,128)(2,1)S(1)}, bf16[3,1024,512]{2,1,0:T(8,128)(2,1)}, u32[]{:S(2)}) copy-start(bf16[3,1024,512]{2,1,0:T(8,128)(2,1)} %param.4) | copy-start | bytes 9437188
  7.2 80.0 %all-gather.2.cloned.1.call-start = ((), (), s32[]{:S(2)}) async-start(), calls=%async_computation.6 | async-start | bytes 3244032 | tf_op jit(solution)/shard_map/all_gather | solution.py:130
  9.8 19.9 %all-to-all-start = ((f32[32,1,64]{2,1,0:T(1,128)}), f32[32,1,64]{2,1,0:T(1,128)S(1)}, u32[]{:S(2)}, u32[]{:S(2)}) async-start(f32[32,1,64]{2,1,0:T(1,128)} %broadcast_in_dim.11), calls=%async_computation | async-start | bytes 32768 | tf_op jit(solution)/shard_map/all_to_all | solution.py:13
  24.4 1.7 copy-start.3
  87.2 2.8 %copy-start.2 = (bf16[3,1024,512]{2,1,0:T(8,128)(2,1)S(1)}, bf16[3,1024,512]{2,1,0:T(8,128)(2,1)}, u32[]{:S(2)}) copy-start(bf16[3,1024,512]{2,1,0:T(8,128)(2,1)} %all-gather.2.cloned.1.call-done) | copy-start | bytes 9437188
  87.2 3.8 %copy-start.4 = (bf16[3,1024,512]{2,1,0:T(8,128)(2,1)S(1)}, bf16[3,1024,512]{2,1,0:T(8,128)(2,1)}, u32[]{:S(2)}) copy-start(bf16[3,1024,512]{2,1,0:T(8,128)(2,1)} %copy-done.3) | copy-start | bytes 9437188
  107.7 37.7 %copy-start.6 = (f32[1024,64]{0,1:T(8,128)S(1)}, f32[1024,64]{0,1:T(8,128)}, u32[]{:S(2)}) copy-start(f32[1024,64]{0,1:T(8,128)} %param.5) | copy-start | bytes 786436
  143.5 1.9 copy-start
  182.0 10.8 %all-to-all-start.3 = ((f32[4,1,64]{2,1,0:T(1,128)}), f32[4,1,64]{2,1,0:T(1,128)S(1)}, u32[]{:S(2)}, u32[]{:S(2)}) async-start(f32[4,1,64]{2,1,0:T(1,128)} %broadcast_in_dim.14), calls=%async_computation.3 | async-start | bytes 4096 | tf_op jit(solution)/shard_map/all_to_all | solution.py:13
  192.8 7.2 %all-to-all-start.4 = ((f32[4,1,4096]{2,1,0:T(1,128)}), f32[4,1,4096]{2,1,0:T(1,128)S(1)}, u32[]{:S(2)}, u32[]{:S(2)}) async-start(f32[4,1,4096]{2,1,0:T(1,128)} %reshape.92), calls=%async_computation.4 | async-start | bytes 131072 | tf_op jit(solution)/shard_map/all_to_all | solution.py:13
  214.5 23.7 %copy-start.5 = (f32[1024,64]{0,1:T(8,128)}, f32[1024,64]{0,1:T(8,128)S(1)}, u32[]{:S(2)}) copy-start(f32[1024,64]{0,1:T(8,128)S(1)} %fusion.53) | copy-start | bytes 786436
Sparse Core Ops, SparseCore 0:
  11.1 76.0 all-gather.1
where the time goes:
time: 248 us; the launch traced here: 247 us
  waiting for transfers between devices  65.3 us (26%)
  other arithmetic  60.1 us (24%)
  blocking collectives  44.6 us (18%)
  matrix products  30.1 us (12%)
  starting transfers between devices  23.1 us (9%)
  between operations  14.3 us (6%)
  local copies, waits for them, and re-layouts  9.61 us (4%)
    all_gather x1, waiting for transfers between devices, body(): lax.all_gather(row_coords, 'col', axis=1, tiled=True)  57.4 us
    reduce_sum x1, other arithmetic, body(): jnp.sum(dist, axis=1)  35.8 us
    all_to_all x2, blocking collectives, from_everyone(): return lax.all_to_all(copies, axis, split_axis=0, concat_axis=0, tiled=True)  30.3 us
    all_to_all x3, starting transfers between devices, from_everyone(): return lax.all_to_all(copies, axis, split_axis=0, concat_axis=0, tiled=True)  23 us
    dot_general x1, matrix products, body(): jnp.einsum('ark,bck->abrc', rows, cols, preferred_element_type=jnp.float32)  16 us
    all_to_all x1, blocking collectives, sum_at_owner(): lax.all_to_all(pieces, axis, split_axis=0, concat_axis=0, tiled=True)  14.3 us
    all_to_all x3, waiting for transfers between devices, from_everyone(): return lax.all_to_all(copies, axis, split_axis=0, concat_axis=0, tiled=True)  7.21 us
    dot_general x1, matrix products, body(): jnp.dot(dist, start_block - block_mean[None, :], precision=highest)  6.79 us
  transfers between devices with their start and end apart: 4, of which 4 were waited for; matrix products, arithmetic and copies ran while one was open for 3% of the time, Pallas kernels for 0%

commit v1 on v0

--- a/solution.py
+++ b/solution.py
@@ -127,7 +127,11 @@
 def body(row_coords, col_coords, start_block):
     highest = lax.Precision.HIGHEST
     cols, col_norm = centre_frames(col_coords)
-    rows, row_norm = centre_frames(lax.all_gather(row_coords, "col", axis=1, tiled=True))
+    rows, row_norm = centre_frames(
+        jnp.concatenate(
+            lax.all_to_all(jnp.stack([row_coords] * lax.axis_size("col")), "col", 0, 0), axis=1
+        )
+    )
     cross = jnp.einsum("ark,bck->abrc", rows, cols, preferred_element_type=jnp.float32) / ATOMS
     dist = squared_rmsd(cross, row_norm[:, None], col_norm[None, :])
     row_count, col_count = dist.shape

time: 248 us -> 227 us (0.915)
  waiting for transfers between devices: 65.3 us -> 37.7 us
  blocking collectives: 44.6 us -> 70.2 us
  between operations: 14.3 us -> 0.94 us
  starting transfers between devices: 23.1 us -> 15.8 us
  local copies, waits for them, and re-layouts: 9.61 us -> 12.8 us
    all_gather x1 -> x0, waiting for transfers between devices: 57.4 us -> none  [body(): lax.all_gather(row_coords, 'col', axis=1, tiled=True)]
    all_to_all x0 -> x1, waiting for transfers between devices: none -> 33.5 us  [body(): lax.all_to_all(jnp.stack([row_coords] * lax.axis_size('col')), 'col', 0, 0)]
    all_to_all x2 -> x3, blocking collectives: 30.3 us -> 50.1 us  [from_everyone(): return lax.all_to_all(copies, axis, split_axis=0, concat_axis=0, tiled=True)]
    all_to_all x3 -> x2, starting transfers between devices: 23 us -> 11.7 us  [from_everyone(): return lax.all_to_all(copies, axis, split_axis=0, concat_axis=0, tiled=True)]
    all_to_all x1, blocking collectives: 14.3 us -> 20.1 us  [sum_at_owner(): lax.all_to_all(pieces, axis, split_axis=0, concat_axis=0, tiled=True)]
    all_to_all x0 -> x1, starting transfers between devices: none -> 4.07 us  [body(): lax.all_to_all(jnp.stack([row_coords] * lax.axis_size('col')), 'col', 0, 0)]
    another operation x0 -> x1, local copies, waits for them, and re-layouts: none -> 2.98 us  [body(): jnp.stack([row_coords] * lax.axis_size('col'))]
    all_to_all x3 -> x2, waiting for transfers between devices: 7.21 us -> 4.24 us  [from_everyone(): return lax.all_to_all(copies, axis, split_axis=0, concat_axis=0, tiled=True)]
  transfers between devices with their start and end apart: 4 -> 3, of which waited for: 4 -> 3; matrix products, arithmetic and copies ran while one was open for 3% -> 3% of each run, Pallas kernels for 0% -> 0%
where the time goes in v1:
time: 227 us
  blocking collectives  70.2 us (31%)
  other arithmetic  59.1 us (26%)
  waiting for transfers between devices  37.7 us (17%)
  matrix products  30.1 us (13%)
  starting transfers between devices  15.8 us (7%)
  local copies, waits for them, and re-layouts  12.8 us (6%)
    all_to_all x3, blocking collectives, from_everyone(): return lax.all_to_all(copies, axis, split_axis=0, concat_axis=0, tiled=True)  50.1 us
    reduce_sum x1, other arithmetic, body(): jnp.sum(dist, axis=1)  35.8 us
    all_to_all x1, waiting for transfers between devices, body(): lax.all_to_all(jnp.stack([row_coords] * lax.axis_size('col')), 'col', 0, 0)  33.5 us
    all_to_all x1, blocking collectives, sum_at_owner(): lax.all_to_all(pieces, axis, split_axis=0, concat_axis=0, tiled=True)  20.1 us
    dot_general x1, matrix products, body(): jnp.einsum('ark,bck->abrc', rows, cols, preferred_element_type=jnp.float32)  16 us
    all_to_all x2, starting transfers between devices, from_everyone(): return lax.all_to_all(copies, axis, split_axis=0, concat_axis=0, tiled=True)  11.7 us
    dot_general x1, matrix products, body(): jnp.dot(dist, start_block - block_mean[None, :], precision=highest)  6.79 us
    another operation x3, other arithmetic, body(): lower = jnp.linalg.cholesky(gram)  6.52 us
  transfers between devices with their start and end apart: 3, of which 3 were waited for; matrix products, arithmetic and copies ran while one was open for 3% of the time, Pallas kernels for 0%

profile of v1, /device:TPU:1, one launch (start us, length us, event | category | flops | bytes accessed | tf_op | source)
XLA Modules:
  0.0 226.6 jit_solution(1028833591679327602)
XLA Ops:
  0.6 1.1 reduce_sum.112
  1.7 19.8 %all_to_all.43 = f32[32,1,64]{2,1,0:T(1,128)S(1)} all-to-all(f32[32,1,64]{2,1,0:T(1,128)S(1)} %broadcast_in_dim.11), channel_id=1, replica_groups=mesh['row'=4,'col'=32] {'col'}, dimensions={0} | all-to-all | bytes 16384 | tf_op jit(solution)/shard_map/all_to_all | solution.py:13
  21.5 3.0 %stack.2 = bf16[32,3,32,512]{3,2,1,0:T(8,128)(2,1)} broadcast(bf16[3,32,512]{2,1,0:T(8,128)(2,1)} %param.3), dimensions={1,2,3} | broadcast | bytes 3244032 | tf_op jit(solution)/shard_map/stack | solution.py:132
  24.5 4.1 %all-to-all-start = ((bf16[32,3,32,512]{3,2,1,0:T(8,128)(2,1)}), bf16[32,3,32,512]{3,2,1,0:T(8,128)(2,1)S(1)}, u32[]{:S(2)}, u32[]{:S(2)}) async-start(bf16[32,3,32,512]{3,2,1,0:T(8,128)(2,1)} %stack.2), calls=%async_computation | async-start | bytes 6291456 | tf_op jit(solution)/shard_map/all_to_all | solution.py:132
  28.6 0.0 copy-start.1
  28.6 2.5 %convert_reduce_fusion = f32[3,1024]{1,0:T(4,128)S(1)} fusion(bf16[3,1024,512]{2,1,0:T(8,128)(2,1)} %param.4), kind=kLoop, calls=%fused_computation.11 | loop fusion | flops 3142656 | bytes 3158016 | tf_op jit(solution)/shard_map/reduce_sum | solution.py:72
  31.1 0.3 copy-done.1
  31.4 0.8 fusion.6
  32.2 0.0 copy-start.2
  32.2 1.7 copy-done.2
  33.9 0.7 multiply_reduce_fusion
  34.6 33.5 %all-to-all-done = bf16[32,3,32,512]{3,2,1,0:T(8,128)(2,1)S(1)} async-done(((bf16[32,3,32,512]{3,2,1,0:T(8,128)(2,1)}), bf16[32,3,32,512]{3,2,1,0:T(8,128)(2,1)S(1)}, u32[]{:S(2)}, u32[]{:S(2)}) %all-to-all-start) | async-done | bytes 3145760 | tf_op jit(solution)/shard_map/all_to_all | solution.py:132
  68.0 0.5 fusion.53
  68.6 0.1 div.88
  68.7 0.9 copy_convert_fusion
  69.6 0.0 copy-start.3
  69.6 1.0 fusion.7
  70.6 0.9 copy-done.3
  71.5 16.0 %multiply_bitcast_fusion = f32[3,3,1024,1024]{2,3,0,1:T(8,128)} fusion(bf16[3,1024,512]{2,1,0:T(8,128)(2,1)S(1)} %copy-done.3, bf16[3,1024,512]{2,1,0:T(8,128)(2,1)S(1)} %fusion.7), kind=kOutput, calls=%fused_computation | convolution fusion | flops 9673113600 | bytes 44040192 | tf_op jit(solution)/shard_map/ark,bck->abrc/dot_general | solution.py:135
  87.5 0.7 multiply_reduce_fusion.1
  88.2 0.0 copy-start.5
  88.2 35.8 %fusion.70 = (f32[1024]{0:T(1024)S(1)}, f32[1024,1024]{0,1:T(8,128)S(1)}) fusion(f32[3,3,1024,1024]{2,3,0,1:T(8,128)} %multiply_bitcast_fusion, f32[1024]{0:T(1024)S(1)} %get-tuple-element.14, f32[1024]{0:T(1024)S(1)} %get-tuple-element.15), kind=kLoop, calls=%fused_computation.120 | loop fusion | flops 210762752 | bytes 41955328 | tf_op jit(solution)/shard_map/reduce_sum | solution.py:143
  124.0 0.0 copy-start
  124.0 1.9 copy-done
  125.9 0.0 copy-done.5
  125.9 6.8 %fusion.62 = f32[1024,64]{1,0:T(8,128)S(1)} fusion(f32[1024,1024]{0,1:T(8,128)S(1)} %get-tuple-element.13, f32[1024,64]{0,1:T(8,128)S(1)} %copy-done.5, f32[64]{0:T(128)S(1)} %broadcast_multiply_fusion.4), kind=kOutput, calls=%fused_computation.97 | convolution fusion | flops 805371904 | bytes 4718848 | tf_op jit(solution)/shard_map/dot_general | solution.py:142
  132.7 0.1 reshape.94
  132.9 0.4 all_to_all.30
  133.3 20.1 %all_to_all.44 = f32[32,1,2080]{2,1,0:T(1,128)S(1)} all-to-all(f32[32,1,2080]{2,1,0:T(1,128)S(1)} %all_to_all.30), channel_id=1, replica_groups=mesh['row'=4,'col'=32] {'col'}, dimensions={0} | all-to-all | bytes 532480 | tf_op jit(solution)/shard_map/all_to_all | solution.py:44
  153.4 0.2 reduce_sum.115
  153.5 0.1 broadcast_in_dim.12
  153.7 12.9 %all_to_all.45 = f32[32,1,2080]{2,1,0:T(1,128)S(1)} all-to-all(f32[32,1,2080]{2,1,0:T(1,128)S(1)} %broadcast_in_dim.12), channel_id=1, replica_groups=mesh['row'=4,'col'=32] {'col'}, dimensions={0} | all-to-all | bytes 532480 | tf_op jit(solution)/shard_map/all_to_all | solution.py:13
  166.6 0.7 reduce.12
  167.3 0.2 slice.69
  167.5 0.2 slice_reduce_fusion
  167.7 0.6 broadcast_in_dim.14
  168.3 7.8 %all-to-all-start.4 = ((f32[4,1,64]{2,1,0:T(1,128)}), f32[4,1,64]{2,1,0:T(1,128)S(1)}, u32[]{:S(2)}, u32[]{:S(2)}) async-start(f32[4,1,64]{2,1,0:T(1,128)} %broadcast_in_dim.14), calls=%async_computation.4 | async-start | bytes 4096 | tf_op jit(solution)/shard_map/all_to_all | solution.py:13
  176.0 1.0 fusion.57
  177.0 0.2 reshape.96
  177.3 0.8 reshape.105
  178.0 1.0 all-to-all-done.4
  179.0 3.9 %all-to-all-start.5 = ((f32[4,1,4096]{2,1,0:T(1,128)}), f32[4,1,4096]{2,1,0:T(1,128)S(1)}, u32[]{:S(2)}, u32[]{:S(2)}) async-start(f32[4,1,4096]{2,1,0:T(1,128)} %reshape.105), calls=%async_computation.5 | async-start | bytes 131072 | tf_op jit(solution)/shard_map/all_to_all | solution.py:13
  183.0 3.2 %all-to-all-done.5 = f32[4,1,4096]{2,1,0:T(1,128)S(1)} async-done(((f32[4,1,4096]{2,1,0:T(1,128)}), f32[4,1,4096]{2,1,0:T(1,128)S(1)}, u32[]{:S(2)}, u32[]{:S(2)}) %all-to-all-start.5) | async-done | bytes 65568 | tf_op jit(solution)/shard_map/all_to_all | solution.py:13
  186.2 0.5 broadcast.156
  186.8 0.8 reduce.14
  187.6 0.1 reshape.106
  187.7 0.1 copy.77
  187.8 0.1 fusion.67
  187.9 5.8 %cholesky.16 = f32[64,64]{1,0:T(8,128)S(1)} custom-call(f32[64,64]{1,0:T(8,128)S(1)} %fusion.67), custom_call_target="Cholesky" | custom-call | tf_op jit(solution)/shard_map/jit(cholesky)/cholesky | solution.py:154
  193.8 0.6 compare_reduce_fusion
  194.4 0.7 fusion.65
  195.1 4.9 %custom-call.6 = f32[1,64,64]{1,2,0:T(8,128)S(1)} custom-call(f32[1,64,64]{2,1,0:T(8,128)S(1)} %fusion.65), custom_call_target="InvertDiagBlocksLowerTriangular" | custom-call | tf_op jit(solution)/shard_map/triangular_solve | solution.py:155
  200.0 0.8 fusion.54
  200.8 0.0 copy-start.4
  200.8 5.3 %fusion.71 = f32[1024,64]{1,0:T(8,128)S(1)} fusion(f32[1024,1024]{0,1:T(8,128)} %copy-done, f32[1024,64]{0,1:T(8,128)S(1)} %fusion.54), kind=kOutput, calls=%fused_computation.121 | convolution fusion | flops 805306368 | bytes 4718592 | tf_op jit(solution)/shard_map/dot_general | solution.py:158
  206.0 0.3 convolution_bitcast_fusion
  206.3 0.2 reshape.95
  206.5 0.5 broadcast_in_dim.30
  207.1 17.3 %all_to_all.46 = f32[4,1,65600]{2,1,0:T(1,128)S(1)} all-to-all(f32[4,1,65600]{2,1,0:T(1,128)S(1)} %broadcast_in_dim.30), channel_id=1, replica_groups=mesh['row'=4,'col'=32] {'row'}, dimensions={0} | all-to-all | bytes 2099200 | tf_op jit(solution)/shard_map/all_to_all | solution.py:13
  224.4 0.0 copy-done.4
  224.4 1.0 reduce_sum.119
  225.5 0.1 reshape.97
  225.7 0.9 copy.80
  (18 shorter events, 0.2 us)
Async XLA Ops:
  24.5 43.6 %all-to-all-start = ((bf16[32,3,32,512]{3,2,1,0:T(8,128)(2,1)}), bf16[32,3,32,512]{3,2,1,0:T(8,128)(2,1)S(1)}, u32[]{:S(2)}, u32[]{:S(2)}) async-start(bf16[32,3,32,512]{3,2,1,0:T(8,128)(2,1)} %stack.2), calls=%async_computation | async-start | bytes 6291456 | tf_op jit(solution)/shard_map/all_to_all | solution.py:132
  28.6 2.8 %copy-start.1 = (bf16[3,1024,512]{2,1,0:T(8,128)(2,1)S(1)}, bf16[3,1024,512]{2,1,0:T(8,128)(2,1)}, u32[]{:S(2)}) copy-start(bf16[3,1024,512]{2,1,0:T(8,128)(2,1)} %param.4) | copy-start | bytes 9437188
  32.2 1.7 copy-start.2
  69.6 1.9 copy-start.3
  88.2 37.7 %copy-start.5 = (f32[1024,64]{0,1:T(8,128)S(1)}, f32[1024,64]{0,1:T(8,128)}, u32[]{:S(2)}) copy-start(f32[1024,64]{0,1:T(8,128)} %param.5) | copy-start | bytes 786436
  124.0 1.9 copy-start
  168.3 10.8 %all-to-all-start.4 = ((f32[4,1,64]{2,1,0:T(1,128)}), f32[4,1,64]{2,1,0:T(1,128)S(1)}, u32[]{:S(2)}, u32[]{:S(2)}) async-start(f32[4,1,64]{2,1,0:T(1,128)} %broadcast_in_dim.14), calls=%async_computation.4 | async-start | bytes 4096 | tf_op jit(solution)/shard_map/all_to_all | solution.py:13
  179.0 7.2 %all-to-all-start.5 = ((f32[4,1,4096]{2,1,0:T(1,128)}), f32[4,1,4096]{2,1,0:T(1,128)S(1)}, u32[]{:S(2)}, u32[]{:S(2)}) async-start(f32[4,1,4096]{2,1,0:T(1,128)} %reshape.105), calls=%async_computation.5 | async-start | bytes 131072 | tf_op jit(solution)/shard_map/all_to_all | solution.py:13
  200.8 23.7 %copy-start.4 = (f32[1024,64]{0,1:T(8,128)}, f32[1024,64]{0,1:T(8,128)S(1)}, u32[]{:S(2)}) copy-start(f32[1024,64]{0,1:T(8,128)S(1)} %fusion.54) | copy-start | bytes 786436
